TPU v7x, 32 devices: a whole 2x2x4 slice. The times are simulated.
32 devices in a mesh: dp: 8 (over y, x, core), mp: 4 (over z).
Axes of the slice: x: 2, y: 2, z: 4, core: 2. Of those that a mesh axis runs over, the one named last changes fastest.
Arguments:
- tokens: bfloat16 [320, 4096], P('dp'), may hold values from -6 to 6
- attn_gain: float32 [4096], replicated, may hold values from 0.1 to 1.9
- head_gain: float32 [4096], replicated, may hold values from 0.1 to 1.9
- qkv_weight: bfloat16 [4096, 3, 4096], P('dp', None, 'mp'), may hold values from -0.09375 to 0.09375
- out_weight: bfloat16 [4096, 4096], P('mp', 'dp'), may hold values from -0.09375 to 0.09375
- head_weight: bfloat16 [4096, 1024], P('mp'), may hold values from -0.09375 to 0.09375
- key_cache: bfloat16 [320, 64, 4096], P('dp', None, 'mp'), may hold values from -400 to 400
- value_cache: bfloat16 [320, 64, 4096], P('dp', None, 'mp'), may hold values from -6 to 6
- parents: int32 [320], P('dp'), may hold values from 0 to 19
- allowed: int32 [320, 2], P('dp'), may hold values from 0 to 7, all different within a row
Outputs:
- new_stream: bfloat16 [320, 4096], P('dp')
- next_logits: float32 [320, 256], P('dp', 'mp')
Inputs may be any that keep to these rules, and one draw needn't show every extreme that they name: `parents`: a beam's parent is a beam of the same query. `allowed`: the 2 block ids of a beam differ.
All inputs are finite; a program needn't handle non-finite values.
Results may differ from a plain program's by a relative error of at most 0.017.
Values may be sent and summed in bfloat16 or wider, within the bound.
No kernel may reach another device: no remote copies, remote signals or barrier semaphores. Data moves between devices by JAX's collectives and lax.ppermute only.
A program may use at most 128 MiB of HBM per device.

v0:
```python
import jax
import jax.numpy as jnp
from jax import lax
from jax.sharding import PartitionSpec as P

HEAD = 128
BEAMS = 20
BLOCK = 128


def root_norm(values, gain_vec):
    float_values = values.astype(jnp.float32)
    factor = lax.rsqrt(jnp.mean(float_values * float_values, axis=-1, keepdims=True) + 1e-06)
    return float_values * factor * gain_vec


def select_blocks(whole_logits, allowed):
    block_count = whole_logits.shape[1] // BLOCK
    block_list = whole_logits.reshape(whole_logits.shape[0], block_count, BLOCK)
    one_hot_rows = (
        allowed[:, :, None] == jnp.arange(block_count, dtype=jnp.int32)[None, None, :]
    ).astype(jnp.float32)
    selected_token = jnp.einsum(
        "ioh,ihp->iop", one_hot_rows, block_list, precision=lax.Precision.HIGHEST
    )
    return selected_token.reshape(whole_logits.shape[0], -1)


def on_device(
    tokens,
    attn_gain,
    head_gain,
    qkv_weight,
    out_weight,
    head_weight,
    key_cache,
    value_cache,
    parents,
    allowed,
):
    row_count = tokens.shape[0]
    normed = root_norm(tokens, attn_gain).astype(jnp.bfloat16)
    spread = lax.all_to_all(normed, "dp", split_axis=1, concat_axis=0, tiled=True)
    depth_part = qkv_weight.shape[0]
    head_width = qkv_weight.shape[2]
    flat_qkv = qkv_weight.reshape(depth_part, 3 * head_width)
    projected = lax.psum_scatter(
        jnp.dot(spread, flat_qkv, preferred_element_type=jnp.float32),
        "dp",
        scatter_dimension=0,
        tiled=True,
    )
    projected = projected.astype(jnp.bfloat16).reshape(row_count, 3, head_width)
    local_heads = head_width // HEAD
    length = key_cache.shape[1] + 1
    source = jnp.arange(row_count, dtype=jnp.int32) // BEAMS * BEAMS + parents
    key_rows = jnp.concatenate(
        [jnp.take(key_cache, source, axis=0), projected[:, 1][:, None]], axis=1
    )
    value_rows = jnp.concatenate(
        [jnp.take(value_cache, source, axis=0), projected[:, 2][:, None]], axis=1
    )
    key_rows = key_rows.reshape(row_count, length, local_heads, HEAD)
    value_rows = value_rows.reshape(row_count, length, local_heads, HEAD)
    queries = projected[:, 0].reshape(row_count, local_heads, HEAD)
    scores = jnp.einsum(
        "thd,tjhd->thj", queries, key_rows, preferred_element_type=jnp.float32
    ) * HEAD ** (-0.5)
    softmax_w = jax.nn.softmax(scores, axis=-1).astype(jnp.bfloat16)
    attention_result = jnp.einsum(
        "thj,tjhd->thd", softmax_w, value_rows, preferred_element_type=jnp.float32
    )
    attention_result = attention_result.astype(jnp.bfloat16).reshape(row_count, head_width)
    partial_value = jnp.dot(
        attention_result,
        lax.all_gather(out_weight, "dp", axis=1, tiled=True),
        preferred_element_type=jnp.float32,
    )
    attn_out = lax.psum(partial_value, "mp")
    stream = tokens.astype(jnp.float32) + attn_out
    head_input = root_norm(stream, head_gain).astype(jnp.bfloat16)
    depth_rows = head_weight.shape[0]
    own_part = lax.dynamic_slice_in_dim(
        head_input, lax.axis_index("mp") * depth_rows, depth_rows, 1
    )
    partial_logits = jnp.dot(own_part, head_weight, preferred_element_type=jnp.float32)
    next_logits = lax.psum_scatter(
        select_blocks(partial_logits, allowed).astype(jnp.bfloat16),
        "mp",
        scatter_dimension=1,
        tiled=True,
    ).astype(jnp.float32)
    return (stream.astype(jnp.bfloat16), next_logits)


def solution(mesh):
    in_specs = (
        P("dp", None),
        P(),
        P(),
        P("dp", None, "mp"),
        P("mp", "dp"),
        P("mp", None),
        P("dp", None, "mp"),
        P("dp", None, "mp"),
        P("dp"),
        P("dp", None),
    )
    out_specs = (P("dp", None), P("dp", "mp"))
    return jax.shard_map(
        on_device, mesh=mesh, in_specs=in_specs, out_specs=out_specs, check_vma=False
    )
```

profile of v0, /device:TPU:0, one launch (start us, length us, event | category | flops | bytes accessed | tf_op | source)
XLA Modules:
  0.0 211.9 jit_solution(16103499963755374255)
XLA Ops:
  7.2 1.3 fusion.11
  8.5 1.1 fusion.13
  9.6 0.7 copy.55
  10.4 5.2 %all-to-all-start = ((bf16[40,8,512]{2,0,1:T(8,128)(2,1)}), bf16[40,8,512]{2,0,1:T(8,128)(2,1)S(1)}, u32[]{:S(2)}, u32[]{:S(2)}) async-start(bf16[40,8,512]{2,0,1:T(8,128)(2,1)} %bitcast.32), calls=%async_computation | async-start | bytes 655360 | tf_op jit(solution)/shard_map/all_to_all | solution.py:43
  15.6 4.7 %copy.24 = bf16[512,3,1024]{0,2,1:T(8,128)(2,1)} copy(bf16[512,3,1024]{2,0,1:T(8,128)(2,1)} %param.15) | data formatting | bytes 6291456 | tf_op args[3]
  20.3 2.9 %all-to-all-done = bf16[40,8,512]{2,0,1:T(8,128)(2,1)S(1)} async-done(((bf16[40,8,512]{2,0,1:T(8,128)(2,1)}), bf16[40,8,512]{2,0,1:T(8,128)(2,1)S(1)}, u32[]{:S(2)}, u32[]{:S(2)}) %all-to-all-start) | async-done | bytes 327712 | tf_op jit(solution)/shard_map/all_to_all | solution.py:43
  23.2 5.0 %fusion.35 = f32[320,3072]{1,0:T(8,128)} fusion(bf16[320,512]{1,0:T(8,128)(2,1)S(1)} %bitcast.34, bf16[512,3072]{0,1:T(8,128)(2,1)} %bitcast.33), kind=kOutput, calls=%fused_computation.57 | convolution fusion | flops 1006632960 | bytes 7405568 | tf_op jit(solution)/shard_map/dot_general | solution.py:48
  29.1 7.2 %gather_fusion = bf16[40,64,1024]{2,1,0:T(8,128)(2,1)} fusion(bf16[40,64,1024]{2,1,0:T(8,128)(2,1)} %param.18, s32[1024]{0:T(1024)S(1)} %pad_clamp_fusion), kind=kCustom, calls=%fused_computation.clone | custom fusion | bytes 10485920 | tf_op jit(solution)/shard_map/jit(_take)/gather | solution.py:58
  36.3 7.6 %gather_fusion.1 = bf16[40,64,1024]{2,1,0:T(8,128)(2,1)} fusion(bf16[40,64,1024]{2,1,0:T(8,128)(2,1)} %param.19, s32[1024]{0:T(1024)S(1)} %pad_clamp_fusion), kind=kCustom, calls=%fused_computation.1.clone | custom fusion | bytes 10485920 | tf_op jit(solution)/shard_map/jit(_take)/gather | solution.py:61
  43.9 9.1 %broadcast_select_fusion.1 = (bf16[40,64,1024]{2,1,0:T(8,128)(2,1)}, bf16[40,64,1024]{2,1,0:T(8,128)(2,1)}) fusion(bf16[40,64,1024]{2,1,0:T(8,128)(2,1)} %gather_fusion, pred[40]{0:T(512)(128)(4,1)S(1)} %get-tuple-element.5, bf16[40,64,1024]{2,1,0:T(8,128)(2,1)} %gather_fusion.1), kind=kLoop, calls=%fused_computation.11 | loop fusion | flops 5242880 | bytes 20971560 | tf_op jit(solution)/shard_map/jit(_take)/select_n | solution.py:58
  52.9 24.6 %reduce-scatter.5.cloned.1.call-done = f32[40,3072]{1,0:T(8,128)} async-done(((f32[320,3072]{1,0:T(8,128)}), f32[40,3072]{1,0:T(8,128)}) %reduce-scatter.5.cloned.1.call-update) | async-done | bytes 491536 | tf_op jit(solution)/shard_map/reduce_scatter | solution.py:47
  77.6 1.1 convert_element_type.34
  79.3 11.1 %pad_maximum_fusion = (bf16[40,65,1024]{2,1,0:T(8,128)(2,1)}, bf16[40,65,1024]{2,1,0:T(8,128)(2,1)}) fusion(bf16[40,1,1024]{2,1,0:T(2,128)(2,1)S(1)} %get-tuple-element.7, bf16[40,64,1024]{2,1,0:T(8,128)(2,1)} %get-tuple-element.9, bf16[40,1,1024]{2,1,0:T(2,128)(2,1)S(1)} %get-tuple-element.8, bf16[40,64,1024]{2,1,0:T(8,128)(2,1)} %get-tuple-element.10), kind=kLoop, calls=%fused_computation.4 | loop fusion | flops 21299200 | bytes 21299200 | tf_op jit(solution)/shard_map/concatenate | solution.py:57
  90.4 9.1 %reshape.86 = bf16[40,65,8,128]{3,2,1,0:T(8,128)(2,1)} reshape(bf16[40,65,1024]{2,1,0:T(8,128)(2,1)} %get-tuple-element.11) | data formatting | bytes 10649600 | tf_op jit(solution)/shard_map/reshape | solution.py:63
  99.5 9.3 %reshape.87 = bf16[40,65,8,128]{3,2,1,0:T(8,128)(2,1)} reshape(bf16[40,65,1024]{2,1,0:T(8,128)(2,1)} %get-tuple-element.12) | data formatting | bytes 10649600 | tf_op jit(solution)/shard_map/reshape | solution.py:64
  108.8 5.9 %fusion.4 = f32[40,8,1,65]{3,2,1,0:T(1,128)S(1)} fusion(bf16[40,65,8,128]{3,2,1,0:T(8,128)(2,1)} %reshape.86, bf16[40,3,1024]{2,1,0:T(4,128)(2,1)S(1)} %reshape.54), kind=kOutput, calls=%fused_computation.8 | convolution fusion | flops 5324800 | bytes 5571840 | tf_op jit(solution)/shard_map/thd,tjhd->thj/dot_general | solution.py:66
  114.9 4.2 %fusion.2 = f32[40,8,1,128]{3,2,1,0:T(1,128)S(1)} fusion(bf16[40,65,8,128]{3,2,1,0:T(8,128)(2,1)} %reshape.87, bf16[40,8,65,1]{2,1,0,3:T(8,128)(2,1)S(1)} %fusion.10), kind=kOutput, calls=%fused_computation.6 | convolution fusion | flops 5324800 | bytes 5530240 | tf_op jit(solution)/shard_map/thj,tjhd->thd/dot_general | solution.py:70
  119.1 16.2 %all-gather.2.cloned.1.call-done = bf16[1024,4096]{1,0:T(8,128)(2,1)} async-done(((bf16[1024,512]{1,0:T(8,128)(2,1)}), bf16[1024,4096]{1,0:T(8,128)(2,1)}) %all-gather.2.cloned.1.call-update) | async-done | bytes 8388624 | tf_op jit(solution)/shard_map/all_gather | solution.py:76
  135.3 5.9 %fusion.19 = f32[40,4096]{1,0:T(8,128)} fusion(bf16[1024,4096]{1,0:T(8,128)(2,1)} %all-gather.2.cloned.1.call-done, bf16[5,8,8,128]{3,2,1,0:T(8,128)(2,1)S(1)} %bitcast.36), kind=kOutput, calls=%fused_computation.34 | convolution fusion | flops 335544320 | bytes 9125888 | tf_op jit(solution)/shard_map/dot_general | solution.py:74
  142.1 39.9 %all-reduce.2.cloned.1.call-done = f32[40,4096]{1,0:T(8,128)} async-done(((f32[40,4096]{1,0:T(8,128)}), f32[40,4096]{1,0:T(8,128)}) %all-reduce.2.cloned.1.call-update) | async-done | bytes 655376 | tf_op jit(solution)/shard_map/psum | solution.py:79
  181.9 1.3 multiply_reduce_fusion
  184.9 0.8 convert_element_type.37
  185.7 18.2 %reduce-scatter.7.cloned.1.call-done = bf16[64,40]{1,0:T(8,128)(2,1)} async-done(((bf16[256,40]{1,0:T(8,128)(2,1)}), bf16[64,40]{1,0:T(8,128)(2,1)}) %reduce-scatter.7.cloned.1.call-update) | async-done | bytes 5136
  203.9 0.8 copy.39
  (31 shorter events, 4.9 us)
Async XLA Ops:
  7.2 176.1 %copy-start = (bf16[1024,1024]{1,0:T(8,128)(2,1)S(1)}, bf16[1024,1024]{1,0:T(8,128)(2,1)}, u32[]{:S(2)}) copy-start(bf16[1024,1024]{1,0:T(8,128)(2,1)} %param.17) | copy-start | bytes 6291460
  10.4 12.8 %all-to-all-start = ((bf16[40,8,512]{2,0,1:T(8,128)(2,1)}), bf16[40,8,512]{2,0,1:T(8,128)(2,1)S(1)}, u32[]{:S(2)}, u32[]{:S(2)}) async-start(bf16[40,8,512]{2,0,1:T(8,128)(2,1)} %bitcast.32), calls=%async_computation | async-start | bytes 655360 | tf_op jit(solution)/shard_map/all_to_all | solution.py:43
  15.6 62.0 %reduce-scatter.5.cloned.1.call-start = ((), (), s32[]{:S(2)}) async-start(), calls=%async_computation.3 | async-start | bytes 4423680 | tf_op jit(solution)/shard_map/reduce_scatter | solution.py:47
  23.2 5.8 %copy-start.3 = (s32[40]{0:T(128)S(1)}, s32[40]{0:T(128)}, u32[]{:S(2)}) copy-start(s32[40]{0:T(128)} %param.20) | copy-start | bytes 484
  28.2 107.1 %all-gather.2.cloned.1.call-start = ((), (), s32[]{:S(2)}) async-start(), calls=%async_computation.4 | async-start | bytes 9437184 | tf_op jit(solution)/shard_map/all_gather | solution.py:76
  29.0 153.0 %all-reduce.2.cloned.1.call-start = ((), (), s32[]{:S(2)}) async-start(), calls=%async_computation.5 | async-start | bytes 1310720 | tf_op jit(solution)/shard_map/psum | solution.py:79
  135.3 6.0 %copy-start.2 = (s32[40,2]{0,1:T(2,128)S(1)}, s32[40,2]{0,1:T(2,128)}, u32[]{:S(2)}) copy-start(s32[40,2]{0,1:T(2,128)} %param.21) | copy-start | bytes 964
  135.3 46.6 %copy-start.1 = (bf16[40,4096]{1,0:T(8,128)(2,1)S(1)}, bf16[40,4096]{1,0:T(8,128)(2,1)}, u32[]{:S(2)}) copy-start(bf16[40,4096]{1,0:T(8,128)(2,1)} %param.12) | copy-start | bytes 983044
  141.2 62.7 %reduce-scatter.7.cloned.1.call-start = ((), (), s32[]{:S(2)}) async-start(), calls=%async_computation.6 | async-start | bytes 81920
Sparse Core Ops, SparseCore 0:
  28.3 49.1 reduce-scatter.4
  79.4 55.8 all-gather.1
  141.4 40.5 all-reduce.1
  185.0 18.8 reduce-scatter.6
where the time goes:
time: 213 us; the launch traced here: 212 us
  waiting for transfers between devices  103 us (48%)
  local copies, waits for them, and re-layouts  41.6 us (20%)
  other arithmetic  26.6 us (12%)
  matrix products  21.8 us (10%)
  between operations  13.9 us (7%)
  starting transfers between devices  5.36 us (3%)
    psum x1, waiting for transfers between devices, on_device(): attn_out = lax.psum(partial_value, 'mp')  39.9 us
    reduce_scatter x1, waiting for transfers between devices, on_device(): lax.psum_scatter(jnp.dot(spread, flat_qkv, preferred_element_type=jnp.flo...  24.6 us
    unnamed x5, waiting for transfers between devices  19 us
    all_gather x1, waiting for transfers between devices, on_device(): lax.all_gather(out_weight, 'dp', axis=1, tiled=True)  16.2 us
    concatenate x1, other arithmetic, on_device(): jnp.concatenate([jnp.take(key_cache, source, axis=0), projected[:, 1][:,...  11.1 us
    reshape x1, local copies, waits for them, and re-layouts, on_device(): value_rows = value_rows.reshape(row_count, length, local_heads, HEAD)  9.25 us
    reshape x1, local copies, waits for them, and re-layouts, on_device(): key_rows = key_rows.reshape(row_count, length, local_heads, HEAD)  9.11 us
    select_n x1, other arithmetic, on_device(): jnp.take(key_cache, source, axis=0)  9.08 us
  transfers between devices with their start and end apart: 5, of which 5 were waited for; matrix products, arithmetic and copies ran while one was open for 34% of the time, Pallas kernels for 0%

commit v1 on v0

--- a/solution.py
+++ b/solution.py
@@ -76,7 +76,9 @@
         lax.all_gather(out_weight, "dp", axis=1, tiled=True),
         preferred_element_type=jnp.float32,
     )
-    attn_out = lax.psum(partial_value, "mp")
+    attn_out = partial_value
+    for hop in (1, 2):
+        attn_out = attn_out + lax.ppermute(attn_out, "mp", [(dev, dev ^ hop) for dev in range(4)])
     stream = tokens.astype(jnp.float32) + attn_out
     head_input = root_norm(stream, head_gain).astype(jnp.bfloat16)
     depth_rows = head_weight.shape[0]

time: 213 us -> 220 us (1.033)
  starting transfers between devices: 5.36 us -> 9.32 us
  waiting for transfers between devices: 103 us -> 106 us
    ppermute x0 -> x2, waiting for transfers between devices: none -> 43.3 us  [on_device(): lax.ppermute(attn_out, 'mp', [(dev, dev ^ hop) for dev in range(4)])]
    psum x1 -> x0, waiting for transfers between devices: 39.9 us -> none  [on_device(): attn_out = lax.psum(partial_value, 'mp')]
    ppermute x0 -> x2, starting transfers between devices: none -> 4.01 us  [on_device(): lax.ppermute(attn_out, 'mp', [(dev, dev ^ hop) for dev in range(4)])]
    unnamed x5 -> x4, waiting for transfers between devices: 19 us -> 19.4 us
    unnamed x13 -> x15, local copies, waits for them, and re-layouts: 6.34 us -> 6.34 us
  transfers between devices with their start and end apart: 5 -> 6, of which waited for: 5 -> 6; matrix products, arithmetic and copies ran while one was open for 34% -> 33% of each run, Pallas kernels for 0% -> 0%
where the time goes in v1:
time: 220 us; the launch traced here: 219 us
  waiting for transfers between devices  106 us (48%)
  local copies, waits for them, and re-layouts  41.6 us (19%)
  other arithmetic  26.9 us (12%)
  matrix products  20.9 us (10%)
  between operations  13.9 us (6%)
  starting transfers between devices  9.32 us (4%)
    ppermute x2, waiting for transfers between devices, on_device(): lax.ppermute(attn_out, 'mp', [(dev, dev ^ hop) for dev in range(4)])  43.3 us
    reduce_scatter x1, waiting for transfers between devices, on_device(): lax.psum_scatter(jnp.dot(spread, flat_qkv, preferred_element_type=jnp.flo...  24.6 us
    unnamed x4, waiting for transfers between devices  19.4 us
    all_gather x1, waiting for transfers between devices, on_device(): lax.all_gather(out_weight, 'dp', axis=1, tiled=True)  16.2 us
    concatenate x1, other arithmetic, on_device(): jnp.concatenate([jnp.take(key_cache, source, axis=0), projected[:, 1][:,...  11.1 us
    reshape x1, local copies, waits for them, and re-layouts, on_device(): value_rows = value_rows.reshape(row_count, length, local_heads, HEAD)  9.25 us
    reshape x1, local copies, waits for them, and re-layouts, on_device(): key_rows = key_rows.reshape(row_count, length, local_heads, HEAD)  9.12 us
    select_n x1, other arithmetic, on_device(): jnp.take(key_cache, source, axis=0)  9.08 us
  transfers between devices with their start and end apart: 6, of which 6 were waited for; matrix products, arithmetic and copies ran while one was open for 33% of the time, Pallas kernels for 0%

profile of v1, /device:TPU:0, one launch (start us, length us, event | category | flops | bytes accessed | tf_op | source)
XLA Modules:
  0.0 219.0 jit_solution(15246667602047859498)
XLA Ops:
  7.2 1.3 fusion.11
  8.5 1.1 fusion.13
  10.4 5.2 %all-to-all-start = ((bf16[40,8,512]{2,0,1:T(8,128)(2,1)}), bf16[40,8,512]{2,0,1:T(8,128)(2,1)S(1)}, u32[]{:S(2)}, u32[]{:S(2)}) async-start(bf16[40,8,512]{2,0,1:T(8,128)(2,1)} %bitcast.32), calls=%async_computation | async-start | bytes 655360 | tf_op jit(solution)/shard_map/all_to_all | solution.py:43
  15.6 4.7 %copy.24 = bf16[512,3,1024]{0,2,1:T(8,128)(2,1)} copy(bf16[512,3,1024]{2,0,1:T(8,128)(2,1)} %param.15) | data formatting | bytes 6291456 | tf_op args[3]
  20.3 2.9 %all-to-all-done = bf16[40,8,512]{2,0,1:T(8,128)(2,1)S(1)} async-done(((bf16[40,8,512]{2,0,1:T(8,128)(2,1)}), bf16[40,8,512]{2,0,1:T(8,128)(2,1)S(1)}, u32[]{:S(2)}, u32[]{:S(2)}) %all-to-all-start) | async-done | bytes 327712 | tf_op jit(solution)/shard_map/all_to_all | solution.py:43
  23.2 5.0 %fusion.35 = f32[320,3072]{1,0:T(8,128)} fusion(bf16[320,512]{1,0:T(8,128)(2,1)S(1)} %bitcast.34, bf16[512,3072]{0,1:T(8,128)(2,1)} %bitcast.33), kind=kOutput, calls=%fused_computation.57 | convolution fusion | flops 1006632960 | bytes 7405568 | tf_op jit(solution)/shard_map/dot_general | solution.py:48
  29.0 7.2 %gather_fusion = bf16[40,64,1024]{2,1,0:T(8,128)(2,1)} fusion(bf16[40,64,1024]{2,1,0:T(8,128)(2,1)} %param.18, s32[1024]{0:T(1024)S(1)} %pad_clamp_fusion), kind=kCustom, calls=%fused_computation.clone | custom fusion | bytes 10485920 | tf_op jit(solution)/shard_map/jit(_take)/gather | solution.py:58
  36.3 7.6 %gather_fusion.1 = bf16[40,64,1024]{2,1,0:T(8,128)(2,1)} fusion(bf16[40,64,1024]{2,1,0:T(8,128)(2,1)} %param.19, s32[1024]{0:T(1024)S(1)} %pad_clamp_fusion), kind=kCustom, calls=%fused_computation.1.clone | custom fusion | bytes 10485920 | tf_op jit(solution)/shard_map/jit(_take)/gather | solution.py:61
  43.9 9.1 %broadcast_select_fusion.1 = (bf16[40,64,1024]{2,1,0:T(8,128)(2,1)}, bf16[40,64,1024]{2,1,0:T(8,128)(2,1)}) fusion(bf16[40,64,1024]{2,1,0:T(8,128)(2,1)} %gather_fusion, pred[40]{0:T(512)(128)(4,1)S(1)} %get-tuple-element.5, bf16[40,64,1024]{2,1,0:T(8,128)(2,1)} %gather_fusion.1), kind=kLoop, calls=%fused_computation.11 | loop fusion | flops 5242880 | bytes 20971560 | tf_op jit(solution)/shard_map/jit(_take)/select_n | solution.py:58
  52.9 24.6 %reduce-scatter.5.cloned.1.call-done = f32[40,3072]{1,0:T(8,128)} async-done(((f32[320,3072]{1,0:T(8,128)}), f32[40,3072]{1,0:T(8,128)}) %reduce-scatter.5.cloned.1.call-update) | async-done | bytes 491536 | tf_op jit(solution)/shard_map/reduce_scatter | solution.py:47
  77.6 1.1 convert_element_type.34
  79.3 11.1 %pad_maximum_fusion = (bf16[40,65,1024]{2,1,0:T(8,128)(2,1)}, bf16[40,65,1024]{2,1,0:T(8,128)(2,1)}) fusion(bf16[40,1,1024]{2,1,0:T(2,128)(2,1)S(1)} %get-tuple-element.7, bf16[40,64,1024]{2,1,0:T(8,128)(2,1)} %get-tuple-element.9, bf16[40,1,1024]{2,1,0:T(2,128)(2,1)S(1)} %get-tuple-element.8, bf16[40,64,1024]{2,1,0:T(8,128)(2,1)} %get-tuple-element.10), kind=kLoop, calls=%fused_computation.4 | loop fusion | flops 21299200 | bytes 21299200 | tf_op jit(solution)/shard_map/concatenate | solution.py:57
  90.4 9.1 %reshape.86 = bf16[40,65,8,128]{3,2,1,0:T(8,128)(2,1)} reshape(bf16[40,65,1024]{2,1,0:T(8,128)(2,1)} %get-tuple-element.11) | data formatting | bytes 10649600 | tf_op jit(solution)/shard_map/reshape | solution.py:63
  99.5 9.3 %reshape.87 = bf16[40,65,8,128]{3,2,1,0:T(8,128)(2,1)} reshape(bf16[40,65,1024]{2,1,0:T(8,128)(2,1)} %get-tuple-element.12) | data formatting | bytes 10649600 | tf_op jit(solution)/shard_map/reshape | solution.py:64
  108.8 5.9 %fusion.4 = f32[40,8,1,65]{3,2,1,0:T(1,128)S(1)} fusion(bf16[40,65,8,128]{3,2,1,0:T(8,128)(2,1)} %reshape.86, bf16[40,3,1024]{2,1,0:T(4,128)(2,1)S(1)} %reshape.54), kind=kOutput, calls=%fused_computation.8 | convolution fusion | flops 5324800 | bytes 5571840 | tf_op jit(solution)/shard_map/thd,tjhd->thj/dot_general | solution.py:66
  114.9 4.2 %fusion.2 = f32[40,8,1,128]{3,2,1,0:T(1,128)S(1)} fusion(bf16[40,65,8,128]{3,2,1,0:T(8,128)(2,1)} %reshape.87, bf16[40,8,65,1]{2,1,0,3:T(8,128)(2,1)S(1)} %fusion.10), kind=kOutput, calls=%fused_computation.6 | convolution fusion | flops 5324800 | bytes 5530240 | tf_op jit(solution)/shard_map/thj,tjhd->thd/dot_general | solution.py:70
  119.1 16.2 %all-gather.2.cloned.1.call-done = bf16[1024,4096]{1,0:T(8,128)(2,1)} async-done(((bf16[1024,512]{1,0:T(8,128)(2,1)}), bf16[1024,4096]{1,0:T(8,128)(2,1)}) %all-gather.2.cloned.1.call-update) | async-done | bytes 8388624 | tf_op jit(solution)/shard_map/all_gather | solution.py:76
  135.3 5.0 %fusion.19 = f32[40,4096]{1,0:T(8,128)S(1)} fusion(bf16[1024,4096]{1,0:T(8,128)(2,1)} %all-gather.2.cloned.1.call-done, bf16[5,8,8,128]{3,2,1,0:T(8,128)(2,1)S(1)} %bitcast.36), kind=kOutput, calls=%fused_computation.34 | convolution fusion | flops 335544320 | bytes 9125888 | tf_op jit(solution)/shard_map/dot_general | solution.py:74
  140.3 1.5 collective-permute-start
  141.8 15.4 %collective-permute-done = f32[40,4096]{1,0:T(8,128)S(1)} collective-permute-done((f32[40,4096]{1,0:T(8,128)S(1)}, f32[40,4096]{1,0:T(8,128)S(1)}, u32[]{:S(2)}, u32[]{:S(2)}) %collective-permute-start) | collective-permute-done | bytes 655392 | tf_op jit(solution)/shard_map/ppermute | solution.py:81
  157.3 2.5 %collective-permute-start.1 = (f32[40,4096]{1,0:T(8,128)S(1)}, f32[40,4096]{1,0:T(8,128)}, u32[]{:S(2)}, u32[]{:S(2)}) collective-permute-start(f32[40,4096]{1,0:T(8,128)S(1)} %add.44), channel_id=1, source_target_pairs={{0,2},{1,3},{2,0},{3,1},{4,6},{5,7},{6,4},{7,5},{8,10},{9,11},{10,... | collective-permute-start | bytes 1966088 | tf_op jit(solution)/shard_map/ppermute | solution.py:81
  160.6 27.9 %collective-permute-done.1 = f32[40,4096]{1,0:T(8,128)} collective-permute-done((f32[40,4096]{1,0:T(8,128)S(1)}, f32[40,4096]{1,0:T(8,128)}, u32[]{:S(2)}, u32[]{:S(2)}) %collective-permute-start.1) | collective-permute-done | bytes 655392 | tf_op jit(solution)/shard_map/ppermute | solution.py:81
  188.5 1.5 multiply_reduce_fusion
  192.4 18.7 %reduce-scatter.7.cloned.1.call-done = bf16[64,40]{1,0:T(8,128)(2,1)} async-done(((bf16[256,40]{1,0:T(8,128)(2,1)}), bf16[64,40]{1,0:T(8,128)(2,1)}) %reduce-scatter.7.cloned.1.call-update) | async-done | bytes 5136
  (35 shorter events, 7.2 us)
Async XLA Ops:
  7.2 182.8 %copy-start = (bf16[1024,1024]{1,0:T(8,128)(2,1)S(1)}, bf16[1024,1024]{1,0:T(8,128)(2,1)}, u32[]{:S(2)}) copy-start(bf16[1024,1024]{1,0:T(8,128)(2,1)} %param.17) | copy-start | bytes 6291460
  10.4 12.8 %all-to-all-start = ((bf16[40,8,512]{2,0,1:T(8,128)(2,1)}), bf16[40,8,512]{2,0,1:T(8,128)(2,1)S(1)}, u32[]{:S(2)}, u32[]{:S(2)}) async-start(bf16[40,8,512]{2,0,1:T(8,128)(2,1)} %bitcast.32), calls=%async_computation | async-start | bytes 655360 | tf_op jit(solution)/shard_map/all_to_all | solution.py:43
  15.6 62.0 %reduce-scatter.5.cloned.1.call-start = ((), (), s32[]{:S(2)}) async-start(), calls=%async_computation.3 | async-start | bytes 4423680 | tf_op jit(solution)/shard_map/reduce_scatter | solution.py:47
  23.2 5.8 %copy-start.4 = (s32[40]{0:T(128)S(1)}, s32[40]{0:T(128)}, u32[]{:S(2)}) copy-start(s32[40]{0:T(128)} %param.20) | copy-start | bytes 484
  28.2 107.1 %all-gather.2.cloned.1.call-start = ((), (), s32[]{:S(2)}) async-start(), calls=%async_computation.4 | async-start | bytes 9437184 | tf_op jit(solution)/shard_map/all_gather | solution.py:76
  29.0 182.1 %reduce-scatter.7.cloned.1.call-start = ((), (), s32[]{:S(2)}) async-start(), calls=%async_computation.5 | async-start | bytes 81920
  135.3 24.5 %copy-start.3 = (s32[40,2]{0,1:T(2,128)S(1)}, s32[40,2]{0,1:T(2,128)}, u32[]{:S(2)}) copy-start(s32[40,2]{0,1:T(2,128)} %param.21) | copy-start | bytes 964
  135.3 53.1 %copy-start.1 = (bf16[40,4096]{1,0:T(8,128)(2,1)S(1)}, bf16[40,4096]{1,0:T(8,128)(2,1)}, u32[]{:S(2)}) copy-start(bf16[40,4096]{1,0:T(8,128)(2,1)} %param.12) | copy-start | bytes 983044
  140.3 16.9 %collective-permute-start = (f32[40,4096]{1,0:T(8,128)S(1)}, f32[40,4096]{1,0:T(8,128)S(1)}, u32[]{:S(2)}, u32[]{:S(2)}) collective-permute-start(f32[40,4096]{1,0:T(8,128)S(1)} %fusion.19), channel_id=1, source_target_pairs={{0,1},{1,0},{2,3},{3,2},{4,5},{5,4},{6,7},{7,6},{8,9},{9,8},{10,11... | collective-permute-start | bytes 1966088 | tf_op jit(solution)/shard_map/ppermute | solution.py:81
  157.3 3.3 %copy-start.2 = (f32[40,4096]{1,0:T(8,128)}, f32[40,4096]{1,0:T(8,128)S(1)}, u32[]{:S(2)}) copy-start(f32[40,4096]{1,0:T(8,128)S(1)} %add.44) | copy-start | bytes 1966084
  157.3 31.1 %collective-permute-start.1 = (f32[40,4096]{1,0:T(8,128)S(1)}, f32[40,4096]{1,0:T(8,128)}, u32[]{:S(2)}, u32[]{:S(2)}) collective-permute-start(f32[40,4096]{1,0:T(8,128)S(1)} %add.44), channel_id=1, source_target_pairs={{0,2},{1,3},{2,0},{3,1},{4,6},{5,7},{6,4},{7,5},{8,10},{9,11},{10,... | collective-permute-start | bytes 1966088 | tf_op jit(solution)/shard_map/ppermute | solution.py:81
Sparse Core Ops, SparseCore 0:
  28.3 49.1 reduce-scatter.4
  79.4 55.8 all-gather.1
  191.8 19.2 reduce-scatter.6
